TPU v7x, 32 devices: a whole 2x2x4 slice. The times are simulated.
32 devices in a mesh: groups: 2 (over x), blk: 16 (over z, y, core).
Axes of the slice: x: 2, y: 2, z: 4, core: 2. Of those that a mesh axis runs over, the one named last changes fastest.
Arguments:
- hidden: bfloat16 [32, 512, 640], P(('groups', 'blk')), parts along dimension 0, may hold values from -6 to 6
- query_weight: bfloat16 [16, 2560, 640], P('blk')
- query_gain: float32 [5120], replicated, may hold values from 0.1 to 32
- frame_cache: bfloat16 [32, 2, 8, 2, 16, 640], P(('groups', 'blk')), parts along dimension 0, may hold values from -8.1 to 8.1
- span_kv: bfloat16 [32, 2, 512, 640], P(('groups', 'blk')), parts along dimension 0, may hold values from -8 to 8
- selected: int32 [4, 12], P('groups'), parts along dimension 0, may hold values from 1 to 13, as said below
- owner: int32 [4, 16], P('groups'), parts along dimension 0, may hold values from 0 to 15, each once within a row
Outputs:
- attended: bfloat16 [32, 512, 640], P(('groups', 'blk')), parts along dimension 0
There are 2 independent parts, one for each index of `groups`. A program takes and returns all parts, laid end to end along the dimension named above; an argument that names none is the same for every part. Nothing has to cross between parts.
Inputs may be any that keep to these rules, and one draw needn't show every extreme that they name: `selected`: each row names 12 different frames strictly between the first frame and the last 2; frame 16 - 3 is always among them. Each row of owner names every device of the part once, so a device keeps one frame of every rollout.
All inputs are finite; a program needn't handle non-finite values.
Results may differ from a plain program's by a relative error of at most 0.012.
The roundings to bfloat16 on the way count: a program that leaves them out, or rounds other values in their place, can miss the bound.
Values may be sent and summed in bfloat16 or wider, within the bound.
A program may use at most 64 MiB of HBM per device.

v0:
```python
import jax
import jax.numpy as jnp
from jax import lax
from jax.sharding import PartitionSpec as P

HD = 128
HG = 8


norm_epsilon = 1e-06


def from_partner(block, axis, distance):
    count = lax.axis_size(axis)
    route = []
    for low in range(count):
        high = low | 1 << distance
        if high != low and high < count:
            route += [(low, high), (high, low)]
    return lax.ppermute(block, axis, route)


def passed_along(array, axis, by):
    length = lax.axis_size(axis)
    return lax.ppermute(array, axis, [(i, (i + by) % length) for i in range(length)])


def add_columns(running, features, block_piece, offset):
    columns = lax.dynamic_slice_in_dim(features, offset, block_piece.shape[0], 1)
    return running + jnp.dot(columns, block_piece, preferred_element_type=jnp.float32)


def shards(hidden, query_weight, query_gain, frame_cache, span_kv, selected, owner):
    device = lax.axis_index("blk")
    device_count = lax.axis_size("blk")
    slot_count = device_count // HG
    slot_index = device // HG
    group_index = device % HG
    group_width = hidden.shape[2]
    bit_count = HG.bit_length() - 1
    features = hidden[0]
    for bit_number in range(bit_count):
        partner = from_partner(features, "blk", bit_number)
        upper_half = (group_index >> bit_number) % 2 == 1
        features = jnp.where(
            upper_half,
            jnp.concatenate([partner, features], 1),
            jnp.concatenate([features, partner], 1),
        )
    own_block = query_weight[0]
    block_rows = own_block.shape[0]
    running = jnp.zeros((features.shape[0], group_width), jnp.float32)
    half_rows = block_rows // 2
    first_half = own_block[:half_rows]
    second_half = own_block[half_rows:]
    running = add_columns(running, features, first_half, slot_index * block_rows)
    running = add_columns(running, features, second_half, slot_index * block_rows + half_rows)

    def turn_both(turn_index, loop_state):
        partial_sum, leading, trailing = loop_state
        leading = passed_along(leading, "blk", HG)
        trailing = passed_along(trailing, "blk", -HG)
        earlier = (slot_index - turn_index) % slot_count
        later = (slot_index + turn_index) % slot_count
        partial_sum = add_columns(partial_sum, features, leading, earlier * block_rows)
        partial_sum = add_columns(partial_sum, features, trailing, later * block_rows + half_rows)
        return (partial_sum, leading, trailing)

    running, _, _ = lax.fori_loop(1, slot_count, turn_both, (running, first_half, second_half))
    energy = jnp.sum(running * running, axis=1)
    for bit_number in range(bit_count):
        energy = energy + from_partner(energy, "blk", bit_number)
    row_scale = lax.rsqrt(energy / features.shape[1] + norm_epsilon)
    gain_slice = lax.dynamic_slice_in_dim(query_gain, group_index * group_width, group_width)
    query_rows = (running * row_scale[:, None] * gain_slice).astype(jnp.bfloat16)
    outgoing = frame_cache[0]
    outgoing = outgoing.reshape((-1,) + outgoing.shape[2:])
    incoming = lax.all_to_all(outgoing, "blk", split_axis=0, concat_axis=0, tiled=True)
    frame_count = owner.shape[1]
    window_frames = frame_count // 8
    frame_time = jnp.arange(frame_count, dtype=jnp.int32)
    chosen = (
        (frame_time == 0)
        | (frame_time >= frame_count - window_frames)
        | jnp.any(frame_time[:, None] == selected[slot_index][None, :], axis=1)
    )
    placed = owner[slot_index][:, None] == jnp.arange(device_count, dtype=jnp.int32)[None, :]
    owner_kept = jnp.any(placed & chosen[:, None], axis=0)
    frame_tokens = incoming.shape[2]
    key_rows = jnp.concatenate([incoming[:, 0].reshape(-1, group_width), span_kv[0, 0]], 0)
    value_rows = jnp.concatenate([incoming[:, 1].reshape(-1, group_width), span_kv[0, 1]], 0)
    visible = jnp.concatenate(
        [jnp.repeat(owner_kept, frame_tokens), jnp.ones((query_rows.shape[0],), dtype=bool)]
    )
    head_count = group_width // HD

    def one_head(head_index):
        start = head_index * HD
        query_part = lax.dynamic_slice_in_dim(query_rows, start, HD, 1)
        key_part = lax.dynamic_slice_in_dim(key_rows, start, HD, 1)
        value_part = lax.dynamic_slice_in_dim(value_rows, start, HD, 1)
        scores = lax.dot_general(
            query_part, key_part, (((1,), (1,)), ((), ())), preferred_element_type=jnp.float32
        ) * HD ** (-0.5)
        highest = jnp.max(jnp.where(visible, scores, -jnp.inf), axis=1, keepdims=True)
        probs = jnp.where(visible, jnp.exp(scores - highest), 0.0)
        totals = jnp.sum(probs, axis=1, keepdims=True)
        mixed_rows = jnp.dot(
            probs.astype(jnp.bfloat16), value_part, preferred_element_type=jnp.float32
        )
        return (mixed_rows / totals).astype(jnp.bfloat16)

    head_outputs = lax.map(one_head, jnp.arange(head_count, dtype=jnp.int32))
    return jnp.transpose(head_outputs, (1, 0, 2)).reshape(1, query_rows.shape[0], group_width)


def solution(mesh):
    in_specs = (
        P(("groups", "blk"), None, None),
        P("blk", None, None),
        P(),
        P(("groups", "blk"), None, None, None, None, None),
        P(("groups", "blk"), None, None, None),
        P("groups", None),
        P("groups", None),
    )
    out_specs = P(("groups", "blk"), None, None)
    return jax.shard_map(shards, mesh=mesh, in_specs=in_specs, out_specs=out_specs, check_vma=False)
```

profile of v0, /device:TPU:0, one launch (start us, length us, event | category | flops | bytes accessed | tf_op | source)
XLA Modules:
  0.0 231.8 jit_solution(16575466345846282832)
XLA Ops:
  0.0 0.5 collective-permute-start
  0.5 1.9 collective-permute-done
  2.4 1.7 maximum_select_fusion.2
  4.1 3.0 %collective-permute-start.1 = (bf16[512,1280]{1,0:T(8,128)(2,1)S(1)}, bf16[512,1280]{1,0:T(8,128)(2,1)}, u32[]{:S(2)}, u32[]{:S(2)}) collective-permute-start(bf16[512,1280]{1,0:T(8,128)(2,1)S(1)} %maximum_select_fusion.2), channel_id=1, source_target_pairs={{0,2},{2,0},{1,3},{3,1},{4,6},{6,4},{5,7},{7,5},{8,10},{10,8},{9,1... | collective-permute-start | bytes 3932168 | tf_op jit(solution)/shard_map/ppermute | solution.py:20
  7.0 29.2 %collective-permute-done.1 = bf16[512,1280]{1,0:T(8,128)(2,1)} collective-permute-done((bf16[512,1280]{1,0:T(8,128)(2,1)S(1)}, bf16[512,1280]{1,0:T(8,128)(2,1)}, u32[]{:S(2)}, u32[]{:S(2)}) %collective-permute-start.1) | collective-permute-done | bytes 1310752 | tf_op jit(solution)/shard_map/ppermute | solution.py:20
  36.2 3.0 %maximum_select_fusion.1 = bf16[512,2560]{1,0:T(8,128)(2,1)S(1)} fusion(bf16[512,1280]{1,0:T(8,128)(2,1)} %copy-done.3, bf16[512,1280]{1,0:T(8,128)(2,1)} %collective-permute-done.1, pred[]{:T(512)S(6)} %eq.64), kind=kLoop, calls=%fused_computation.19 | loop fusion | flops 11796480 | bytes 5242881 | tf_op jit(solution)/shard_map/jit(_where)/select_n | solution.py:45
  39.2 1.9 collective-permute-start.2
  41.1 2.0 slice_bitcast_fusion.1
  43.1 2.6 %collective-permute-start.3 = (bf16[1280,640]{1,0:T(8,128)(2,1)}, bf16[1280,640]{1,0:T(8,128)(2,1)}, u32[]{:S(2)}, u32[]{:S(2)}) collective-permute-start(bf16[1280,640]{1,0:T(8,128)(2,1)} %get-tuple-element.80), channel_id=1, source_target_pairs={{0,8},{1,9},{2,10},{3,11},{4,12},{5,13},{6,14},{7,15},{8,0},{9,1},... | collective-permute-start | bytes 4915208 | tf_op jit(solution)/shard_map/while/body/eval_jaxpr/ppermute | solution.py:25
  45.6 0.3 collective-permute-start.4
  46.0 4.9 %all-to-all-start = ((bf16[16,2,16,640]{3,2,1,0:T(8,128)(2,1)}), bf16[16,2,16,640]{3,2,1,0:T(8,128)(2,1)S(1)}, u32[]{:S(2)}, u32[]{:S(2)}) async-start(bf16[16,2,16,640]{3,2,1,0:T(8,128)(2,1)} %bitcast.34), calls=%async_computation | async-start | bytes 1310720 | tf_op jit(solution)/shard_map/all_to_all | solution.py:78
  51.0 0.1 fusion.25
  51.2 2.5 %slice_bitcast_fusion.2 = (bf16[512,640]{1,0:T(8,128)(2,1)}, bf16[512,640]{1,0:T(8,128)(2,1)}) fusion(bf16[1,2,512,640]{3,2,1,0:T(8,128)(2,1)} %param.13), kind=kLoop, calls=%fused_computation.37 | loop fusion | bytes 2621440 | tf_op jit(solution)/shard_map/squeeze | solution.py:91
  53.7 99.3 %collective-permute-done.2 = bf16[512,2560]{1,0:T(8,128)(2,1)} collective-permute-done((bf16[512,2560]{1,0:T(8,128)(2,1)S(1)}, bf16[512,2560]{1,0:T(8,128)(2,1)}, u32[]{:S(2)}, u32[]{:S(2)}) %collective-permute-start.2) | collective-permute-done | bytes 2621472 | tf_op jit(solution)/shard_map/ppermute | solution.py:20
  153.0 4.5 %maximum_select_fusion = bf16[512,5120]{1,0:T(8,128)(2,1)S(1)} fusion(bf16[512,2560]{1,0:T(8,128)(2,1)S(1)} %maximum_select_fusion.1, bf16[512,2560]{1,0:T(8,128)(2,1)} %collective-permute-done.2, pred[]{:T(512)S(6)} %eq.63), kind=kLoop, calls=%fused_computation.18 | loop fusion | flops 23592960 | bytes 10485761 | tf_op jit(solution)/shard_map/jit(_where)/select_n | solution.py:45
  157.6 1.2 fusion.20
  158.8 2.7 %fusion.18 = f32[512,640]{1,0:T(8,128)S(1)} fusion(bf16[1280,640]{1,0:T(8,128)(2,1)} %collective-permute-done.3, bf16[512,5120]{1,0:T(8,128)(2,1)S(1)} %maximum_select_fusion, s32[]{:T(128)S(6)} %select_n.106), kind=kOutput, calls=%fused_computation.30 | convolution fusion | flops 838860800 | bytes 4259844 | tf_op jit(solution)/shard_map/while/body/eval_jaxpr/dot_general | solution.py:30
  161.4 33.9 %collective-permute-done.4 = bf16[1280,640]{1,0:T(8,128)(2,1)} collective-permute-done((bf16[1280,640]{1,0:T(8,128)(2,1)}, bf16[1280,640]{1,0:T(8,128)(2,1)}, u32[]{:S(2)}, u32[]{:S(2)}) %collective-permute-start.4) | collective-permute-done | bytes 1638432 | tf_op jit(solution)/shard_map/while/body/eval_jaxpr/ppermute | solution.py:25
  195.4 2.6 %fusion.16 = f32[512,640]{1,0:T(8,128)S(1)} fusion(bf16[1280,640]{1,0:T(8,128)(2,1)} %collective-permute-done.4, bf16[512,5120]{1,0:T(8,128)(2,1)S(1)} %maximum_select_fusion, s32[]{:T(128)S(6)} %select_n.108), kind=kOutput, calls=%fused_computation.28 | convolution fusion | flops 838860800 | bytes 4259844 | tf_op jit(solution)/shard_map/while/body/eval_jaxpr/dot_general | solution.py:30
  198.0 1.3 multiply_reduce_fusion
  199.3 0.1 collective-permute-start.5
  199.4 0.1 fusion.24
  199.5 0.1 broadcast_in_dim.31
  199.6 0.1 reshape.25
  199.7 0.8 dynamic_slice.42
  200.4 0.1 collective-permute-done.5
  200.5 1.5 collective-permute-start.6
  202.1 0.1 fusion.32
  202.1 2.0 collective-permute-done.6
  204.1 2.3 pad_maximum_fusion
  206.4 1.3 collective-permute-done.7
  207.7 0.2 multiply_convert_fusion
  207.9 21.7 %while.2 = (s32[]{:T(128)}, bf16[5,512,128]{1,2,0:T(8,128)(2,1)}, pred[768]{0:T(1024)(128)(4,1)S(1)}, s32[5]{0:T(128)S(1)}, bf16[512,640]{1,0:T(8,128)(2,1)S(1)}...) while((s32[]{:T(128)}, bf16[5,512,128]{1,2,0:T(8,128)(2,1)}, ...), condition=%wide.region_6.7_spmd, body=%wide.region_3.6_spmd.sunk | while | flops 204995584 | bytes 5912747 | solution.py:113
  207.9 0.6 dynamic_slice.76
  209.2 0.5 select_reduce_fusion.2
  209.7 0.4 fusion.41
  210.1 1.4 fusion.42
  211.5 0.1 copy.20
  211.6 0.7 constant_dynamic-update-slice_fusion.2
  212.3 0.6 dynamic_slice.76
  213.5 0.5 select_reduce_fusion.2
  214.0 0.4 fusion.41
  214.4 1.4 fusion.42
  215.9 0.1 copy.20
  216.0 0.7 constant_dynamic-update-slice_fusion.2
  216.6 0.6 dynamic_slice.76
  217.9 0.5 select_reduce_fusion.2
  218.3 0.4 fusion.41
  218.8 1.4 fusion.42
  220.2 0.1 copy.20
  220.3 0.7 constant_dynamic-update-slice_fusion.2
  221.0 0.6 dynamic_slice.76
  222.2 0.5 select_reduce_fusion.2
  222.7 0.4 fusion.41
  223.1 1.4 fusion.42
  224.5 0.1 copy.20
  224.7 0.7 constant_dynamic-update-slice_fusion.2
  225.3 0.6 dynamic_slice.76
  226.6 0.5 select_reduce_fusion.2
  227.0 0.4 fusion.41
  227.5 1.4 fusion.42
  228.9 0.1 copy.20
  229.0 0.7 constant_dynamic-update-slice_fusion.2
  229.7 2.2 copy.16
  (24 shorter events, 0.1 us)
Async XLA Ops:
  0.0 51.2 %copy-start = (s32[2,16]{1,0:T(2,128)S(1)}, s32[2,16]{1,0:T(2,128)}, u32[]{:S(2)}) copy-start(s32[2,16]{1,0:T(2,128)} %param.15) | copy-start | bytes 388
  0.0 2.4 %collective-permute-start = (bf16[512,640]{1,0:T(8,128)(2,1)}, bf16[512,640]{1,0:T(8,128)(2,1)S(1)}, u32[]{:S(2)}, u32[]{:S(2)}) collective-permute-start(bf16[512,640]{1,0:T(8,128)(2,1)} %bitcast.36), channel_id=1, source_target_pairs={{0,1},{1,0},{2,3},{3,2},{4,5},{5,4},{6,7},{7,6},{8,9},{9,8},{10,11... | collective-permute-start | bytes 1966088 | tf_op jit(solution)/shard_map/ppermute | solution.py:20
  4.1 3.0 %copy-start.3 = (bf16[512,1280]{1,0:T(8,128)(2,1)}, bf16[512,1280]{1,0:T(8,128)(2,1)S(1)}, u32[]{:S(2)}) copy-start(bf16[512,1280]{1,0:T(8,128)(2,1)S(1)} %maximum_select_fusion.2) | copy-start | bytes 3932164
  4.1 32.1 %collective-permute-start.1 = (bf16[512,1280]{1,0:T(8,128)(2,1)S(1)}, bf16[512,1280]{1,0:T(8,128)(2,1)}, u32[]{:S(2)}, u32[]{:S(2)}) collective-permute-start(bf16[512,1280]{1,0:T(8,128)(2,1)S(1)} %maximum_select_fusion.2), channel_id=1, source_target_pairs={{0,2},{2,0},{1,3},{3,1},{4,6},{6,4},{5,7},{7,5},{8,10},{10,8},{9,1... | collective-permute-start | bytes 3932168 | tf_op jit(solution)/shard_map/ppermute | solution.py:20
  7.0 34.0 %copy-start.1 = (bf16[1,2560,640]{2,1,0:T(8,128)(2,1)S(1)}, bf16[1,2560,640]{2,1,0:T(8,128)(2,1)}, u32[]{:S(2)}) copy-start(bf16[1,2560,640]{2,1,0:T(8,128)(2,1)} %param.10) | copy-start | bytes 9830404
  39.2 11.8 %copy-start.5 = (s32[2,12]{1,0:T(2,128)S(1)}, s32[2,12]{1,0:T(2,128)}, u32[]{:S(2)}) copy-start(s32[2,12]{1,0:T(2,128)} %param.14) | copy-start | bytes 292
  39.2 113.8 %collective-permute-start.2 = (bf16[512,2560]{1,0:T(8,128)(2,1)S(1)}, bf16[512,2560]{1,0:T(8,128)(2,1)}, u32[]{:S(2)}, u32[]{:S(2)}) collective-permute-start(bf16[512,2560]{1,0:T(8,128)(2,1)S(1)} %maximum_select_fusion.1), channel_id=1, source_target_pairs={{0,4},{4,0},{1,5},{5,1},{2,6},{6,2},{3,7},{7,3},{8,12},{12,8},{9,1... | collective-permute-start | bytes 7864328 | tf_op jit(solution)/shard_map/ppermute | solution.py:20
  43.1 115.7 %collective-permute-start.3 = (bf16[1280,640]{1,0:T(8,128)(2,1)}, bf16[1280,640]{1,0:T(8,128)(2,1)}, u32[]{:S(2)}, u32[]{:S(2)}) collective-permute-start(bf16[1280,640]{1,0:T(8,128)(2,1)} %get-tuple-element.80), channel_id=1, source_target_pairs={{0,8},{1,9},{2,10},{3,11},{4,12},{5,13},{6,14},{7,15},{8,0},{9,1},... | collective-permute-start | bytes 4915208 | tf_op jit(solution)/shard_map/while/body/eval_jaxpr/ppermute | solution.py:25
  45.6 149.7 %collective-permute-start.4 = (bf16[1280,640]{1,0:T(8,128)(2,1)}, bf16[1280,640]{1,0:T(8,128)(2,1)}, u32[]{:S(2)}, u32[]{:S(2)}) collective-permute-start(bf16[1280,640]{1,0:T(8,128)(2,1)} %get-tuple-element.81), channel_id=1, source_target_pairs={{0,8},{1,9},{2,10},{3,11},{4,12},{5,13},{6,14},{7,15},{8,0},{9,1},... | collective-permute-start | bytes 4915208 | tf_op jit(solution)/shard_map/while/body/eval_jaxpr/ppermute | solution.py:25
  46.0 156.1 %all-to-all-start = ((bf16[16,2,16,640]{3,2,1,0:T(8,128)(2,1)}), bf16[16,2,16,640]{3,2,1,0:T(8,128)(2,1)S(1)}, u32[]{:S(2)}, u32[]{:S(2)}) async-start(bf16[16,2,16,640]{3,2,1,0:T(8,128)(2,1)} %bitcast.34), calls=%async_computation | async-start | bytes 1310720 | tf_op jit(solution)/shard_map/all_to_all | solution.py:78
  53.7 103.9 %copy-start.2 = (bf16[1,2560,640]{2,1,0:T(8,128)(2,1)S(1)}, bf16[1,2560,640]{2,1,0:T(8,128)(2,1)}, u32[]{:S(2)}) copy-start(bf16[1,2560,640]{2,1,0:T(8,128)(2,1)} %param.10) | copy-start | bytes 9830404
  199.3 4.8 %copy-start.4 = (bf16[512,640]{1,0:T(8,128)(2,1)S(1)}, bf16[512,640]{1,0:T(8,128)(2,1)}, u32[]{:S(2)}) copy-start(bf16[512,640]{1,0:T(8,128)(2,1)} %get-tuple-element.82) | copy-start | bytes 1966084
  199.3 1.2 collective-permute-start.5
  200.5 3.6 %collective-permute-start.6 = (f32[512]{0:T(512)S(1)}, f32[512]{0:T(512)S(1)}, u32[]{:S(2)}, u32[]{:S(2)}) collective-permute-start(f32[512]{0:T(512)S(1)} %add.114), channel_id=1, source_target_pairs={{0,2},{2,0},{1,3},{3,1},{4,6},{6,4},{5,7},{7,5},{8,10},{10,8},{9,1... | collective-permute-start | bytes 6152 | tf_op jit(solution)/shard_map/ppermute | solution.py:20
  204.1 3.6 %collective-permute-start.7 = (f32[512]{0:T(512)S(1)}, f32[512]{0:T(512)S(1)}, u32[]{:S(2)}, u32[]{:S(2)}) collective-permute-start(f32[512]{0:T(512)S(1)} %add.115), channel_id=1, source_target_pairs={{0,4},{4,0},{1,5},{5,1},{2,6},{6,2},{3,7},{7,3},{8,12},{12,8},{9,1... | collective-permute-start | bytes 6152 | tf_op jit(solution)/shard_map/ppermute | solution.py:20
where the time goes:
time: 232 us
  waiting for transfers between devices  168 us (72%)
  matrix products  17.2 us (7%)
  starting transfers between devices  14.7 us (6%)
  local copies, waits for them, and re-layouts  14.5 us (6%)
  other arithmetic  14.1 us (6%)
  loops' own time  3.36 us (1%)
    ppermute x6, waiting for transfers between devices, from_partner(): return lax.ppermute(block, axis, route)  134 us
    ppermute x2, waiting for transfers between devices, passed_along(): lax.ppermute(array, axis, [(i, (i + by) % length) for i in range(length)])  33.9 us
    select_n x3, other arithmetic, shards(): jnp.where(upper_half, jnp.concatenate([partner, features], 1), jnp.concat...  9.16 us
    dot_general x4, matrix products, add_columns(): jnp.dot(columns, block_piece, preferred_element_type=jnp.float32)  7.81 us
    dot_general x5, matrix products, one_head(): jnp.dot(probs.astype(jnp.bfloat16), value_part, preferred_element_type=jn...  7.09 us
    ppermute x6, starting transfers between devices, from_partner(): return lax.ppermute(block, axis, route)  6.86 us
    all_to_all x1, starting transfers between devices, shards(): lax.all_to_all(outgoing, 'blk', split_axis=0, concat_axis=0, tiled=True)  4.93 us
  transfers between devices with their start and end apart: 9, of which 7 were waited for; matrix products, arithmetic and copies ran while one was open for 9% of the time, Pallas kernels for 0%

commit v1 on v0

--- a/solution.py
+++ b/solution.py
@@ -1,6 +1,10 @@
+import math
+
 import jax
 import jax.numpy as jnp
 from jax import lax
+from jax.experimental import pallas as pl
+from jax.experimental.pallas import tpu as pltpu
 from jax.sharding import PartitionSpec as P
 
 HD = 128
@@ -114,7 +118,246 @@
     return jnp.transpose(head_outputs, (1, 0, 2)).reshape(1, query_rows.shape[0], group_width)
 
 
+CHUNKS = 5
+MESH = pl.DeviceIdType.MESH
+SPAN_MASKS = ((0, 0), (1, 0), (0, 1), (1, 1))
+
+
+def flipped(index, y_flip, z_flip):
+    if y_flip:
+        index = index + 2 - 4 * ((index // 2) % 2)
+    if z_flip:
+        index = index + 4 - 8 * ((index // 4) % 2)
+    return index
+
+
+def fused_kernel(
+    hidden, weight, gain, frames, span, visible, out,
+    x_all, w_own, w_far, kv_frames, kv_span, total, energy, scale,
+    local_sem, x_send, x_recv, c_send, c_recv, w_send, w_recv, f_send, f_recv,
+    k_send, k_recv, e_send, e_recv,
+):
+    part = lax.axis_index("groups")
+    me = lax.axis_index("blk")
+    count = 2 * HG
+    slot = me // HG
+    group = me % HG
+    rows = weight.shape[1]
+    half = rows // 2
+    chunk = half // CHUNKS
+    width = hidden.shape[2]
+    core_peer = me + 1 - 2 * (me % 2)
+    far = (me + HG) % count
+
+    def columns(block):
+        return x_all.at[:, pl.ds(pl.multiple_of((block % HG) * width, 128), width)]
+
+    locals_ = [
+        pltpu.make_async_copy(hidden.at[0], columns(me), local_sem.at[0]),
+        pltpu.make_async_copy(weight.at[0], w_own, local_sem.at[1]),
+        pltpu.make_async_copy(span.at[0], kv_span, local_sem.at[2]),
+        pltpu.make_async_copy(frames.at[0, slot, group], kv_frames.at[:, me], local_sem.at[3]),
+    ]
+    for copy in locals_:
+        copy.start()
+
+    barrier = pltpu.get_barrier_semaphore()
+
+    def greet(step, carry):
+        pl.semaphore_signal(barrier, inc=1, device_id={"blk": (me + step) % count}, device_id_type=MESH)
+        return carry
+
+    lax.fori_loop(1, count, greet, 0)
+    pl.semaphore_signal(barrier, inc=1, device_id={"groups": 1 - part}, device_id_type=MESH)
+    pl.semaphore_wait(barrier, count)
+
+    def far_copy(k, base):
+        block = pl.ds(pl.multiple_of(base * half + k * chunk, chunk), chunk)
+        return pltpu.make_async_remote_copy(
+            weight.at[0, block], w_far.at[block], w_send.at[k], w_recv.at[k],
+            device_id={"blk": far}, device_id_type=MESH)
+
+    def side_copy(k, base):
+        block = pl.ds(pl.multiple_of(base * half + k * chunk, chunk), chunk)
+        return pltpu.make_async_remote_copy(
+            w_far.at[block], w_far.at[block], f_send.at[k], f_recv.at[k],
+            device_id={"groups": 1 - part}, device_id_type=MESH)
+
+    def span_copy(j):
+        return pltpu.make_async_remote_copy(
+            hidden.at[0], columns(me), x_send.at[j], x_recv.at[j],
+            device_id={"blk": flipped(me, *SPAN_MASKS[j])}, device_id_type=MESH)
+
+    def span_wait(j):
+        block = columns(flipped(me, *SPAN_MASKS[j]))
+        pltpu.make_async_remote_copy(
+            block, block, x_send.at[j], x_recv.at[j],
+            device_id={"blk": flipped(me, *SPAN_MASKS[j])}, device_id_type=MESH).wait_recv()
+
+    def core_copy(j, of):
+        block = columns(flipped(of, *SPAN_MASKS[j]))
+        return pltpu.make_async_remote_copy(
+            hidden.at[0] if j == 0 and of is me else block, block, c_send.at[j], c_recv.at[j],
+            device_id={"blk": core_peer}, device_id_type=MESH)
+
+    def frame_copy(step):
+        to = (me + step) % count
+        return pltpu.make_async_remote_copy(
+            frames.at[0, to // HG, to % HG], kv_frames.at[:, me], k_send.at[step], k_recv.at[step],
+            device_id={"blk": to}, device_id_type=MESH)
+
+    def frame_wait(step):
+        come = (me + count - step) % count
+        pltpu.make_async_remote_copy(
+            kv_frames.at[:, come], kv_frames.at[:, come], k_send.at[step], k_recv.at[step],
+            device_id={"blk": come}, device_id_type=MESH).wait_recv()
+
+    def each(start, stop, act):
+        def body(i, carry):
+            act(i)
+            return carry
+        lax.fori_loop(start, stop, body, 0)
+
+    for j in (1, 2, 3):
+        span_copy(j).start()
+    core_copy(0, me).start()
+    each(0, CHUNKS, lambda k: far_copy(k, part).start())
+    each(1, count, lambda step: frame_copy(step).start())
+    for copy in locals_:
+        copy.wait()
+    for j in (1, 2, 3):
+        span_wait(j)
+        core_copy(j, me).start()
+    for j in range(4):
+        core_copy(j, core_peer).wait_recv()
+
+    total[...] = jnp.zeros_like(total)
+
+    def add(w_ref, offset, row):
+        at = pl.multiple_of(offset + row, 128)
+        total[...] += jnp.dot(
+            x_all[:, pl.ds(at, chunk)], w_ref[pl.ds(pl.multiple_of(row, chunk), chunk), :],
+            preferred_element_type=jnp.float32)
+
+    each(0, rows // chunk, lambda i: add(w_own, slot * rows, i * chunk))
+
+    def arrive(k):
+        far_copy(k, part).wait_recv()
+        side_copy(k, part).start()
+        add(w_far, (1 - slot) * rows, part * half + k * chunk)
+        side_copy(k, 1 - part).wait_recv()
+        add(w_far, (1 - slot) * rows, (1 - part) * half + k * chunk)
+
+    each(0, CHUNKS, arrive)
+
+    query = total[...]
+    sums = jnp.sum(query * query, axis=1, keepdims=True)
+    energy[group] = jnp.transpose(jnp.broadcast_to(sums, (sums.shape[0], 128)))[:8]
+
+    def energy_copy(step):
+        to = (group + step) % HG
+        return pltpu.make_async_remote_copy(
+            energy.at[group], energy.at[group], e_send.at[step], e_recv.at[step],
+            device_id={"blk": slot * HG + to}, device_id_type=MESH)
+
+    def energy_wait(step):
+        come = (group + HG - step) % HG
+        pltpu.make_async_remote_copy(
+            energy.at[come], energy.at[come], e_send.at[step], e_recv.at[step],
+            device_id={"blk": slot * HG + come}, device_id_type=MESH).wait_recv()
+
+    each(1, HG, lambda step: energy_copy(step).start())
+    each(1, count, frame_wait)
+    each(1, HG, energy_wait)
+    mean = jnp.sum(energy[...], axis=0) / (HG * width)
+    row_scale = lax.rsqrt(mean + norm_epsilon)
+    scale[...] = jnp.transpose(jnp.concatenate([row_scale] * 16, axis=0))
+
+    shown = visible[...] > 0.5
+    factor = HD ** (-0.5) * math.log2(math.e)
+    contract = (((1,), (1,)), ((), ()))
+
+    def one_head(h):
+        at = pl.ds(pl.multiple_of(h * HD, HD), HD)
+        query_part = (total[:, at] * scale[...] * gain[:, at]).astype(jnp.bfloat16)
+        key_old = kv_frames[0, :, :, at].reshape(-1, HD)
+        value_old = kv_frames[1, :, :, at].reshape(-1, HD)
+        key_new = kv_span[0, :, at]
+        value_new = kv_span[1, :, at]
+        old = lax.dot_general(query_part, key_old, contract, preferred_element_type=jnp.float32)
+        new = lax.dot_general(query_part, key_new, contract, preferred_element_type=jnp.float32)
+        old = jnp.where(shown, old, -jnp.inf)
+        highest = jnp.maximum(
+            jnp.max(old, axis=1, keepdims=True), jnp.max(new, axis=1, keepdims=True))
+        old = jnp.exp2((old - highest) * factor)
+        new = jnp.exp2((new - highest) * factor)
+        totals = jnp.sum(old, axis=1, keepdims=True) + jnp.sum(new, axis=1, keepdims=True)
+        mixed = jnp.dot(old.astype(jnp.bfloat16), value_old, preferred_element_type=jnp.float32)
+        mixed += jnp.dot(new.astype(jnp.bfloat16), value_new, preferred_element_type=jnp.float32)
+        out[0, :, at] = (mixed / totals).astype(jnp.bfloat16)
+
+    each(0, width // HD, one_head)
+
+    for j in (1, 2, 3):
+        span_copy(j).wait_send()
+    for j in range(4):
+        core_copy(j, me).wait_send()
+    each(0, CHUNKS, lambda k: far_copy(k, part).wait_send())
+    each(0, CHUNKS, lambda k: side_copy(k, part).wait_send())
+    each(1, count, lambda step: frame_copy(step).wait_send())
+    each(1, HG, lambda step: energy_copy(step).wait_send())
+
+
+def fused(hidden, query_weight, query_gain, frame_cache, span_kv, selected, owner):
+    device = lax.axis_index("blk")
+    device_count = lax.axis_size("blk")
+    slot_index = device // HG
+    group_index = device % HG
+    tokens, width = hidden.shape[1:]
+    rows = query_weight.shape[1]
+    frame_tokens = frame_cache.shape[4]
+    frame_count = owner.shape[1]
+    window_frames = frame_count // 8
+    frame_time = jnp.arange(frame_count, dtype=jnp.int32)
+    chosen = (
+        (frame_time == 0)
+        | (frame_time >= frame_count - window_frames)
+        | jnp.any(frame_time[:, None] == selected[slot_index][None, :], axis=1)
+    )
+    placed = owner[slot_index][:, None] == jnp.arange(device_count, dtype=jnp.int32)[None, :]
+    owner_kept = jnp.any(placed & chosen[:, None], axis=0)
+    visible = jnp.repeat(owner_kept, frame_tokens).astype(jnp.float32)[None, :]
+    gain_slice = lax.dynamic_slice_in_dim(query_gain, group_index * width, width)[None, :]
+    dma = pltpu.SemaphoreType.DMA
+    anywhere = pl.BlockSpec(memory_space=pl.ANY)
+    inside = pl.BlockSpec(memory_space=pltpu.VMEM)
+    bf16, f32 = jnp.bfloat16, jnp.float32
+    return pl.pallas_call(
+        fused_kernel,
+        out_shape=jax.ShapeDtypeStruct((1, tokens, width), bf16),
+        in_specs=[anywhere, anywhere, inside, anywhere, anywhere, inside],
+        out_specs=inside,
+        scratch_shapes=[
+            pltpu.VMEM((tokens, HG * width), bf16),
+            pltpu.VMEM((rows, width), bf16),
+            pltpu.VMEM((rows, width), bf16),
+            pltpu.VMEM((2, device_count, frame_tokens, width), bf16),
+            pltpu.VMEM((2, tokens, width), bf16),
+            pltpu.VMEM((tokens, width), f32),
+            pltpu.VMEM((HG, 8, tokens), f32),
+            pltpu.VMEM((tokens, 128), f32),
+            dma((4,)), dma((4,)), dma((4,)), dma((4,)), dma((4,)),
+            dma((CHUNKS,)), dma((CHUNKS,)), dma((CHUNKS,)), dma((CHUNKS,)),
+            dma((device_count,)), dma((device_count,)), dma((HG,)), dma((HG,)),
+        ],
+        compiler_params=pltpu.CompilerParams(
+            collective_id=0, has_side_effects=True, vmem_limit_bytes=48 * 1024 * 1024),
+    )(hidden, query_weight, gain_slice, frame_cache, span_kv, visible)
+
+
 def solution(mesh):
+    small = mesh.shape["blk"] == 2 * HG and mesh.shape["groups"] == 2
+    body = fused if small else shards
     in_specs = (
         P(("groups", "blk"), None, None),
         P("blk", None, None),
@@ -125,4 +368,4 @@
         P("groups", None),
     )
     out_specs = P(("groups", "blk"), None, None)
-    return jax.shard_map(shards, mesh=mesh, in_specs=in_specs, out_specs=out_specs, check_vma=False)
+    return jax.shard_map(body, mesh=mesh, in_specs=in_specs, out_specs=out_specs, check_vma=False)

time: 232 us -> 132 us (0.57)
  waiting for transfers between devices: 168 us -> 0 us
  Pallas kernels: 0 us -> 125 us
  matrix products: 17.2 us -> 0 us
  starting transfers between devices: 14.7 us -> 0 us
  other arithmetic: 14.1 us -> 0.23 us
  local copies, waits for them, and re-layouts: 14.5 us -> 5.98 us
  loops' own time: 3.36 us -> 0 us
    ppermute x8 -> x0, waiting for transfers between devices: 168 us -> none  [the longest x6 134 us: from_partner(): return lax.ppermute(block, axis, route)]
    pallas_call x0 -> x1, Pallas kernels: none -> 125 us  [fused(): pl.pallas_call(fused_kernel, out_shape=jax.ShapeDtypeStruct((1, tokens, w...]
    dot_general x14 -> x0, matrix products: 17.2 us -> none  [the longest x4 7.81 us: add_columns(): jnp.dot(columns, block_piece, preferred_element_type=jnp.float32)]
    ppermute x8 -> x0, starting transfers between devices: 9.78 us -> none  [the longest x6 6.86 us: from_partner(): return lax.ppermute(block, axis, route)]
    select_n x3 -> x0, other arithmetic: 9.16 us -> none  [shards(): jnp.where(upper_half, jnp.concatenate([partner, features], 1), jnp.concat...]
    all_to_all x1 -> x0, starting transfers between devices: 4.93 us -> none  [shards(): lax.all_to_all(outgoing, 'blk', split_axis=0, concat_axis=0, tiled=True)]
    unnamed x12 -> x9, local copies, waits for them, and re-layouts: 0.03 us -> 4.34 us
    dynamic_update_slice x10 -> x0, local copies, waits for them, and re-layouts: 3.89 us -> none  [shards(): head_outputs = lax.map(one_head, jnp.arange(head_count, dtype=jnp.int32))]
  transfers between devices with their start and end apart: 9 -> 0, of which waited for: 7 -> 0; matrix products, arithmetic and copies ran while one was open for 9% -> 0% of each run, Pallas kernels for 0% -> 0%
where the time goes in v1:
time: 132 us; the launch traced here: 131 us
  Pallas kernels  125 us (95%)
  local copies, waits for them, and re-layouts  5.98 us (5%)
    pallas_call x1, Pallas kernels, fused(): pl.pallas_call(fused_kernel, out_shape=jax.ShapeDtypeStruct((1, tokens, w...  125 us
    unnamed x9, local copies, waits for them, and re-layouts  4.34 us

profile of v1, /device:TPU:0, one launch (start us, length us, event | category | flops | bytes accessed | tf_op | source)
XLA Modules:
  0.0 131.3 jit_solution(1579591577637617868)
XLA Ops:
  0.0 0.0 copy-start
  0.0 0.7 dynamic-slice_bitcast_fusion
  0.7 0.0 copy-done
  0.7 0.1 fusion.2
  0.8 0.1 fusion.1
  0.9 0.8 dynamic_slice.9
  1.7 0.1 broadcast_in_dim.5
  1.8 0.1 convert_element_type.15.visible
  1.9 0.0 copy-start.1
  1.9 1.3 %copy-done.1 = bf16[1,2,512,640]{3,2,1,0:T(8,128)(2,1)S(1)} copy-done((bf16[1,2,512,640]{3,2,1,0:T(8,128)(2,1)S(1)}, bf16[1,2,512,640]{3,2,1,0:T(8,128)(2,1)}, u32[]{:S(2)}) %copy-start.1) | copy-done | bytes 1310744
  3.2 0.0 copy-start.2
  3.2 1.1 copy-done.2
  4.3 0.0 copy-start.3
  4.3 1.1 copy-done.3
  5.4 125.0 %shard_map.73 = bf16[1,512,640]{2,1,0:T(8,128)(2,1)S(1)} custom-call(bf16[1,512,640]{2,1,0:T(8,128)(2,1)S(1)} %copy-done.2, bf16[1,2560,640]{2,1,0:T(8,128)(2,1)} %weight.1, f32[1,640]{1,0:T(1,128)S(1)} %broadcast_in_dim.4.gain, bf16[1,2,8,2,16,640]{5,4,3,2,1,0:T(8,128)(2,1)S(1)} %copy-done.3, bf16[1,2,512,640]{3,2,1,0:T(8,128)(2,1)S(1)} %copy-done.1, ...), custom_call_target="tpu_custom_call" | custom-call | tf_op jit(solution)/shard_map/pallas_call | solution.py:335
  130.4 0.8 copy.9
  (4 shorter events, 0.0 us)
Async XLA Ops:
  0.0 0.7 copy-start
  1.9 1.3 %copy-start.1 = (bf16[1,2,512,640]{3,2,1,0:T(8,128)(2,1)S(1)}, bf16[1,2,512,640]{3,2,1,0:T(8,128)(2,1)}, u32[]{:S(2)}) copy-start(bf16[1,2,512,640]{3,2,1,0:T(8,128)(2,1)} %span.1) | copy-start | bytes 3932164
  3.2 1.1 copy-start.2
  4.3 1.1 copy-start.3

commit v2 on v1

--- a/solution.py
+++ b/solution.py
@@ -118,7 +118,9 @@
     return jnp.transpose(head_outputs, (1, 0, 2)).reshape(1, query_rows.shape[0], group_width)
 
 
-CHUNKS = 5
+CHUNKS = 10
+AHEAD = 3
+EARLY = 3
 MESH = pl.DeviceIdType.MESH
 SPAN_MASKS = ((0, 0), (1, 0), (0, 1), (1, 1))
 
@@ -221,10 +223,24 @@
     for j in (1, 2, 3):
         span_copy(j).start()
     core_copy(0, me).start()
-    each(0, CHUNKS, lambda k: far_copy(k, part).start())
-    each(1, count, lambda step: frame_copy(step).start())
+    each(0, AHEAD, lambda k: far_copy(k, part).start())
     for copy in locals_:
         copy.wait()
+
+    def hand_on(k):
+        far_copy(k, part).wait_recv()
+        side_copy(k, part).start()
+        far_copy(k, part).wait_send()
+
+        @pl.when(k < CHUNKS - AHEAD)
+        def _():
+            far_copy(k + AHEAD, part).start()
+
+        @pl.when(k == CHUNKS - AHEAD)
+        def _():
+            each(1, count, lambda step: frame_copy(step).start())
+
+    each(0, EARLY, hand_on)
     for j in (1, 2, 3):
         span_wait(j)
         core_copy(j, me).start()
@@ -233,22 +249,38 @@
 
     total[...] = jnp.zeros_like(total)
 
-    def add(w_ref, offset, row):
+    def add(w_ref, offset, row, depth):
         at = pl.multiple_of(offset + row, 128)
         total[...] += jnp.dot(
-            x_all[:, pl.ds(at, chunk)], w_ref[pl.ds(pl.multiple_of(row, chunk), chunk), :],
+            x_all[:, pl.ds(at, depth)], w_ref[pl.ds(pl.multiple_of(row, depth), depth), :],
             preferred_element_type=jnp.float32)
 
-    each(0, rows // chunk, lambda i: add(w_own, slot * rows, i * chunk))
+    def add_far(k):
+        add(w_far, (1 - slot) * rows, part * half + k * chunk, chunk)
+
+    def add_side(k):
+        side_copy(k, 1 - part).wait_recv()
+        add(w_far, (1 - slot) * rows, (1 - part) * half + k * chunk, chunk)
 
     def arrive(k):
-        far_copy(k, part).wait_recv()
-        side_copy(k, part).start()
-        add(w_far, (1 - slot) * rows, part * half + k * chunk)
-        side_copy(k, 1 - part).wait_recv()
-        add(w_far, (1 - slot) * rows, (1 - part) * half + k * chunk)
-
-    each(0, CHUNKS, arrive)
+        hand_on(k)
+        first = 2 * (k - EARLY)
+
+        @pl.when(first < rows // (2 * chunk))
+        def _():
+            for i in (first, first + 1):
+                add(w_own, slot * rows, i * 2 * chunk, 2 * chunk)
+
+        add_far(k - EARLY)
+        add_side(k - EARLY)
+
+    each(EARLY, CHUNKS, arrive)
+
+    def finish(k):
+        add_far(k)
+        add_side(k)
+
+    each(CHUNKS - EARLY, CHUNKS, finish)
 
     query = total[...]
     sums = jnp.sum(query * query, axis=1, keepdims=True)
@@ -267,12 +299,12 @@
             device_id={"blk": slot * HG + come}, device_id_type=MESH).wait_recv()
 
     each(1, HG, lambda step: energy_copy(step).start())
-    each(1, count, frame_wait)
     each(1, HG, energy_wait)
     mean = jnp.sum(energy[...], axis=0) / (HG * width)
     row_scale = lax.rsqrt(mean + norm_epsilon)
     scale[...] = jnp.transpose(jnp.concatenate([row_scale] * 16, axis=0))
 
+    each(1, count, frame_wait)
     shown = visible[...] > 0.5
     factor = HD ** (-0.5) * math.log2(math.e)
     contract = (((1,), (1,)), ((), ()))
@@ -302,7 +334,6 @@
         span_copy(j).wait_send()
     for j in range(4):
         core_copy(j, me).wait_send()
-    each(0, CHUNKS, lambda k: far_copy(k, part).wait_send())
     each(0, CHUNKS, lambda k: side_copy(k, part).wait_send())
     each(1, count, lambda step: frame_copy(step).wait_send())
     each(1, HG, lambda step: energy_copy(step).wait_send())
@@ -329,7 +360,7 @@
     visible = jnp.repeat(owner_kept, frame_tokens).astype(jnp.float32)[None, :]
     gain_slice = lax.dynamic_slice_in_dim(query_gain, group_index * width, width)[None, :]
     dma = pltpu.SemaphoreType.DMA
-    anywhere = pl.BlockSpec(memory_space=pl.ANY)
+    anywhere = pl.BlockSpec(memory_space=pltpu.HBM)
     inside = pl.BlockSpec(memory_space=pltpu.VMEM)
     bf16, f32 = jnp.bfloat16, jnp.float32
     return pl.pallas_call(

time: 132 us -> 125 us (0.947); the launches traced: 131 us -> 122 us
  Pallas kernels: 125 us -> 116 us
    pallas_call x1, Pallas kernels: 125 us -> 116 us  [fused(): pl.pallas_call(fused_kernel, out_shape=jax.ShapeDtypeStruct((1, tokens, w...]
where the time goes in v2:
time: 125 us; the launch traced here: 122 us
  Pallas kernels  116 us (93%)
  local copies, waits for them, and re-layouts  5.98 us (5%)
    pallas_call x1, Pallas kernels, fused(): pl.pallas_call(fused_kernel, out_shape=jax.ShapeDtypeStruct((1, tokens, w...  116 us
    unnamed x9, local copies, waits for them, and re-layouts  4.34 us

profile of v2, /device:TPU:0, one launch (start us, length us, event | category | flops | bytes accessed | tf_op | source)
XLA Modules:
  0.0 122.1 jit_solution(4310711570833133591)
XLA Ops:
  0.0 0.0 copy-start
  0.0 0.7 dynamic-slice_bitcast_fusion
  0.7 0.0 copy-done
  0.7 0.1 fusion.2
  0.8 0.1 fusion.1
  0.9 0.8 dynamic_slice.9
  1.7 0.1 broadcast_in_dim.5
  1.8 0.1 convert_element_type.15.visible
  1.9 0.0 copy-start.1
  1.9 1.3 %copy-done.1 = bf16[1,2,512,640]{3,2,1,0:T(8,128)(2,1)S(1)} copy-done((bf16[1,2,512,640]{3,2,1,0:T(8,128)(2,1)S(1)}, bf16[1,2,512,640]{3,2,1,0:T(8,128)(2,1)}, u32[]{:S(2)}) %copy-start.1) | copy-done | bytes 1310744
  3.2 0.0 copy-start.2
  3.2 1.1 copy-done.2
  4.3 0.0 copy-start.3
  4.3 1.1 copy-done.3
  5.4 115.9 %shard_map.73 = bf16[1,512,640]{2,1,0:T(8,128)(2,1)S(1)} custom-call(bf16[1,512,640]{2,1,0:T(8,128)(2,1)S(1)} %copy-done.2, bf16[1,2560,640]{2,1,0:T(8,128)(2,1)} %weight.1, f32[1,640]{1,0:T(1,128)S(1)} %broadcast_in_dim.4.gain, bf16[1,2,8,2,16,640]{5,4,3,2,1,0:T(8,128)(2,1)S(1)} %copy-done.3, bf16[1,2,512,640]{3,2,1,0:T(8,128)(2,1)S(1)} %copy-done.1, ...), custom_call_target="tpu_custom_call" | custom-call | tf_op jit(solution)/shard_map/pallas_call | solution.py:366
  121.3 0.8 copy.9
  (4 shorter events, 0.0 us)
Async XLA Ops:
  0.0 0.7 copy-start
  1.9 1.3 %copy-start.1 = (bf16[1,2,512,640]{3,2,1,0:T(8,128)(2,1)S(1)}, bf16[1,2,512,640]{3,2,1,0:T(8,128)(2,1)}, u32[]{:S(2)}) copy-start(bf16[1,2,512,640]{3,2,1,0:T(8,128)(2,1)} %span.1) | copy-start | bytes 3932164
  3.2 1.1 copy-start.2
  4.3 1.1 copy-start.3
